TPU v7x, 32 devices: a whole 2x2x4 slice. The times are simulated.
32 devices in a mesh: row: 8 (over y, x, core), col: 4 (over z).
Axes of the slice: x: 2, y: 2, z: 4, core: 2. Of those that a mesh axis runs over, the one named last changes fastest.
Arguments:
- integrals: float32 [1024, 8, 8192], P(None, 'row', 'col'), may hold values from -6 to 6, as said below
- amplitudes: float32 [1024, 8, 8192], P(None, 'row', 'col'), as said below
- tile_lists: int32 [4, 3], replicated, may hold values from 0 to 3, as said below
- gap_index: int32 [8192], replicated, may hold values from 0 to 511
- pair_gaps: float32 [512], replicated, may hold values from 0.5 to 4
Outputs:
- updated: float32 [1024, 8, 8192], P(None, 'row', 'col')
Inputs may be any that keep to these rules, and one draw needn't show every extreme that they name: `integrals`: symmetric matrix. `amplitudes`: symmetric matrix. `tile_lists`: row t holds 3 distinct tile indices, among them t itself; s appears in row t exactly when t appears in row s.
All inputs are finite; a program needn't handle non-finite values.
Results may differ from a plain program's by a relative error of at most 0.0036.
Values may be sent and summed in bfloat16 or wider, within the bound.
A program may use at most 192 MiB of HBM per device.

v0:
```python
import jax
import jax.numpy as jnp
from jax import lax
from jax.sharding import PartitionSpec as P


def lookup_gaps(indices, pair_gaps):
    table_ids = jnp.arange(pair_gaps.shape[0], dtype=jnp.int32)
    return jnp.sum(
        jnp.where(indices[:, None] == table_ids[None, :], pair_gaps[None, :], 0.0), axis=1
    )


def per_device(integrals, amplitudes, tile_lists, gap_index, pair_gaps):
    rows_here = integrals.shape[0]
    block_width = integrals.shape[2]
    stride = lax.axis_size("row")
    matrix_order = rows_here * stride
    row_place = lax.axis_index("row")
    col_place = lax.axis_index("col")
    tile_count = tile_lists.shape[0]
    per_tile = block_width // stride
    my_list = lax.dynamic_slice_in_dim(tile_lists, col_place, 1, 0)[0]
    local_int = integrals[:, 0, :]
    int_low = local_int.astype(jnp.bfloat16)
    amp_tiles = amplitudes[:, 0, :].astype(jnp.bfloat16).reshape(tile_count, per_tile, block_width)
    compact = amp_tiles[my_list][:, :, None, :]
    amp_strip = lax.all_gather(compact, "row", axis=2, tiled=True)
    selector = (my_list[:, None] == jnp.arange(tile_count, dtype=jnp.int32)[None, :]).astype(
        jnp.bfloat16
    )
    amp_full = jnp.einsum("kt,kjrb->tjrb", selector, amp_strip).reshape(matrix_order, block_width)
    coupled = jnp.dot(
        lax.all_gather(int_low, "col", axis=1, tiled=True),
        amp_full,
        preferred_element_type=jnp.float32,
    )
    pieces = coupled.reshape(rows_here, block_width // stride, stride)
    arrived = lax.all_to_all(pieces, "row", split_axis=2, concat_axis=1, tiled=True)
    stacked = arrived.reshape(rows_here, stride, block_width // stride).reshape(
        matrix_order, block_width // stride
    )
    mirrored = lax.all_to_all(stacked, "col", split_axis=0, concat_axis=1, tiled=True)
    transposed = mirrored.T
    residual = local_int + coupled + transposed
    index_rows = lax.dynamic_slice_in_dim(gap_index.reshape(rows_here, stride), row_place, 1, 1)[
        :, 0
    ]
    index_cols = lax.dynamic_slice_in_dim(gap_index, col_place * block_width, block_width, 0)
    gap_rows = lookup_gaps(index_rows, pair_gaps)
    gap_cols = lookup_gaps(index_cols, pair_gaps)
    updated = -residual / (gap_rows[:, None] + gap_cols[None, :])
    return updated[:, None, :]


def solution(mesh):
    placed = (P(None, "row", "col"), P(None, "row", "col"), P(), P(), P())
    return jax.shard_map(
        per_device, mesh=mesh, in_specs=placed, out_specs=P(None, "row", "col"), check_vma=False
    )
```

profile of v0, /device:TPU:0, one launch (start us, length us, event | category | flops | bytes accessed | tf_op | source)
XLA Modules:
  0.0 829.0 jit_solution(2965992016563527453)
XLA Ops:
  6.5 0.0 all-gather.6.cloned.1.call-start
  6.5 0.7 fusion.7
  7.2 7.1 convert_element_type.11
  14.4 4.6 copy.38
  19.0 4.8 gather_fusion
  23.8 0.0 all-gather.6.cloned.1.call-update
  23.8 0.0 all-gather.4.cloned.1.call-start
  23.9 21.1 %copy.29 = f32[1024,1,2048]{0,2,1:T(8,128)} copy(f32[1024,1,2048]{2,1,0:T(1,128)} %param.5) | data formatting | bytes 16777216 | tf_op args[0]
  45.0 6.0 bitcast_convert_fusion
  51.0 0.0 all-gather.4.cloned.1.call-update
  51.0 0.7 fusion.8
  51.7 100.2 %all-gather.6.cloned.1.call-done = bf16[3,256,16384]{2,1,0:T(8,128)(2,1)} async-done(((bf16[3,256,2048]{2,1,0:T(8,128)(2,1)}), bf16[3,256,16384]{2,1,0:T(8,128)(2,1)}) %all-gather.6.cloned.1.call-update) | async-done | bytes 25165840 | tf_op jit(solution)/shard_map/all_gather | solution.py:28
  151.9 33.0 %copy.30 = bf16[3,256,16384]{1,2,0:T(8,128)(2,1)} copy(bf16[3,256,16384]{2,1,0:T(8,128)(2,1)} %all-gather.6.cloned.1.call-done) | data formatting | bytes 50331648 | tf_op jit(solution)/shard_map/all_gather | solution.py:28
  184.9 53.2 %copy.31 = bf16[3,256,8,2048]{3,0,2,1:T(4,128)(2,1)} copy(bf16[3,256,8,2048]{1,3,2,0:T(8,128)(2,1)} %bitcast.47) | data formatting | bytes 50331648 | tf_op jit(solution)/shard_map/all_gather | solution.py:28
  238.1 30.8 %fusion.4 = bf16[4,256,8,2048]{3,0,2,1:T(4,128)(2,1)} fusion(bf16[3,256,8,2048]{3,0,2,1:T(4,128)(2,1)} %copy.31, s32[3]{0:T(128)S(1)} %fusion.8), kind=kOutput, calls=%fused_computation.16 | convolution fusion | flops 100663312 | bytes 58720268 | tf_op jit(solution)/shard_map/kt,kjrb->tjrb/dot_general | solution.py:32
  268.9 30.0 %copy.32 = bf16[4,256,8,2048]{3,2,1,0:T(8,128)(2,1)} copy(bf16[4,256,8,2048]{3,0,2,1:T(4,128)(2,1)} %fusion.4) | data formatting | bytes 67108864 | tf_op jit(solution)/shard_map/kt,kjrb->tjrb/dot_general | solution.py:32
  298.9 141.4 %all-gather.4.cloned.1.call-done = bf16[1024,8192]{0,1:T(8,128)(2,1)} async-done(((bf16[1024,2048]{0,1:T(8,128)(2,1)}), bf16[1024,8192]{0,1:T(8,128)(2,1)}) %all-gather.4.cloned.1.call-update) | async-done | bytes 16777232 | tf_op jit(solution)/shard_map/all_gather | solution.py:34
  440.3 43.6 %fusion.9 = f32[2048,1024]{1,0:T(8,128)} fusion(bf16[8192,2048]{1,0:T(8,128)(2,1)} %bitcast.50, bf16[1024,8192]{0,1:T(8,128)(2,1)} %all-gather.4.cloned.1.call-done), kind=kOutput, calls=%fused_computation.21 | convolution fusion | flops 34359738368 | bytes 58720256 | tf_op jit(solution)/shard_map/dot_general | solution.py:33
  483.9 9.2 %copy.33 = f32[1024,256,8]{1,0,2:T(8,128)} copy(f32[1024,256,8]{0,2,1:T(8,128)} %bitcast.48) | data formatting | bytes 16777216 | tf_op jit(solution)/shard_map/reshape | solution.py:38
  493.1 97.8 %all_to_all.34 = f32[1024,256,8]{1,0,2:T(8,128)S(1)} all-to-all(f32[1024,256,8]{1,0,2:T(8,128)} %copy.33), channel_id=1, replica_groups=mesh['row'=8,'col'=4] {'row'}, dimensions={2} | all-to-all | bytes 16777216 | tf_op jit(solution)/shard_map/all_to_all | solution.py:39
  590.9 8.1 copy.34
  599.0 0.0 copy-start
  599.0 0.0 copy-start.1
  599.0 5.8 all-to-all-start.1
  604.7 0.0 copy-done
  604.8 0.3 reshape.52
  605.1 0.4 dynamic-slice_reduce_fusion
  605.4 0.0 copy-done.1
  605.5 0.5 select_reduce_fusion.1
  605.9 0.9 select_reduce_fusion
  606.9 180.7 %all-to-all-done.1 = f32[4,2048,256]{2,1,0:T(8,128)} async-done(((f32[4,2048,256]{2,1,0:T(8,128)}), f32[4,2048,256]{2,1,0:T(8,128)}, u32[]{:S(2)}, u32[]{:S(2)}) %all-to-all-start.1) | async-done | bytes 8388640 | tf_op jit(solution)/shard_map/all_to_all | solution.py:43
  787.5 4.4 copy.39
  792.0 9.6 %fusion.2 = f32[1024,1,2048]{0,2,1:T(8,128)} fusion(f32[2048,1024]{1,0:T(8,128)S(1)} %bitcast.49, f32[2048,1024]{1,0:T(8,128)} %fusion.9, f32[1024,1,2048]{0,2,1:T(8,128)} %copy.29, f32[2048]{0:T(1024)S(1)} %select_reduce_fusion, f32[1024]{0:T(1024)S(1)} %select_reduce_fusion.1), kind=kLoop, calls=%fused_computation.4 | loop fusion | flops 10485760 | bytes 33566720 | tf_op jit(solution)/shard_map/broadcast_in_dim | solution.py:53
  801.6 20.5 %copy.36 = f32[1024,1,2048]{2,1,0:T(1,128)} copy(f32[1024,1,2048]{0,2,1:T(8,128)} %fusion.2) | data formatting | bytes 16777216 | tf_op jit(solution)/shard_map/broadcast_in_dim | solution.py:53
  (2 shorter events, 0.0 us)
Async XLA Ops:
  6.5 145.4 %all-gather.6.cloned.1.call-start = ((), (), s32[]{:S(2)}) async-start(), calls=%async_computation.3 | async-start | bytes 28311552 | tf_op jit(solution)/shard_map/all_gather | solution.py:28
  23.8 416.4 %all-gather.4.cloned.1.call-start = ((), (), s32[]{:S(2)}) async-start(), calls=%async_computation.2 | async-start | bytes 20971520 | tf_op jit(solution)/shard_map/all_gather | solution.py:34
  599.0 5.8 copy-start
  599.0 6.5 copy-start.1
  599.0 188.6 %all-to-all-start.1 = ((f32[4,2048,256]{2,1,0:T(8,128)}), f32[4,2048,256]{2,1,0:T(8,128)}, u32[]{:S(2)}, u32[]{:S(2)}) async-start(f32[4,2048,256]{2,1,0:T(8,128)} %bitcast.51), calls=%async_computation.1 | async-start | bytes 16777216 | tf_op jit(solution)/shard_map/all_to_all | solution.py:43
Sparse Core Ops, SparseCore 0:
  24.0 127.9 all-gather.5
  153.5 286.7 all-gather.3
where the time goes:
time: 833 us; the launch traced here: 829 us
  waiting for transfers between devices  422 us (51%)
  local copies, waits for them, and re-layouts  190 us (23%)
  blocking collectives  97.8 us (12%)
  matrix products  74.4 us (9%)
  other arithmetic  24.9 us (3%)
  between operations  13.5 us (2%)
    all_to_all x1, waiting for transfers between devices, per_device(): lax.all_to_all(stacked, 'col', split_axis=0, concat_axis=1, tiled=True)  181 us
    all_gather x1, waiting for transfers between devices, per_device(): lax.all_gather(int_low, 'col', axis=1, tiled=True)  141 us
    all_gather x1, waiting for transfers between devices, per_device(): amp_strip = lax.all_gather(compact, 'row', axis=2, tiled=True)  100 us
    all_to_all x1, blocking collectives, per_device(): lax.all_to_all(pieces, 'row', split_axis=2, concat_axis=1, tiled=True)  97.8 us
    all_gather x2, local copies, waits for them, and re-layouts, per_device(): amp_strip = lax.all_gather(compact, 'row', axis=2, tiled=True)  86.2 us
    dot_general x1, matrix products, per_device(): jnp.dot(lax.all_gather(int_low, 'col', axis=1, tiled=True), amp_full, pre...  43.6 us
    dot_general x1, matrix products, per_device(): jnp.einsum('kt,kjrb->tjrb', selector, amp_strip)  30.8 us
    dot_general x1, local copies, waits for them, and re-layouts, per_device(): jnp.einsum('kt,kjrb->tjrb', selector, amp_strip)  30 us
  transfers between devices with their start and end apart: 3, of which 3 were waited for; matrix products, arithmetic and copies ran while one was open for 21% of the time, Pallas kernels for 0%

commit v1 on v0

--- a/solution.py
+++ b/solution.py
@@ -25,7 +25,24 @@
     int_low = local_int.astype(jnp.bfloat16)
     amp_tiles = amplitudes[:, 0, :].astype(jnp.bfloat16).reshape(tile_count, per_tile, block_width)
     compact = amp_tiles[my_list][:, :, None, :]
-    amp_strip = lax.all_gather(compact, "row", axis=2, tiled=True)
+    size, index, width = (lax.axis_size("row"), lax.axis_index("row"), compact.shape[2])
+    ahead = [(i, (i + 1) % size) for i in range(size)]
+    left = [(i, (i - 1) % size) for i in range(size)]
+    whole = jnp.zeros((*compact.shape[:2], size * width, *compact.shape[2 + 1 :]), compact.dtype)
+    whole = lax.dynamic_update_slice_in_dim(whole, compact, index * width, axis=2)
+    from_left = from_right = compact
+    halfway = size // 2
+    for step in range(1, halfway + 1):
+        from_left = lax.ppermute(from_left, "row", ahead)
+        whole = lax.dynamic_update_slice_in_dim(
+            whole, from_left, (index - step) % size * width, axis=2
+        )
+        if step < size - halfway:
+            from_right = lax.ppermute(from_right, "row", left)
+            whole = lax.dynamic_update_slice_in_dim(
+                whole, from_right, (index + step) % size * width, axis=2
+            )
+    amp_strip = whole
     selector = (my_list[:, None] == jnp.arange(tile_count, dtype=jnp.int32)[None, :]).astype(
         jnp.bfloat16
     )

time: 833 us -> 760 us (0.912)
  waiting for transfers between devices: 422 us -> 356 us
  local copies, waits for them, and re-layouts: 190 us -> 165 us
  starting transfers between devices: 5.82 us -> 15.5 us
    ppermute x0 -> x7, waiting for transfers between devices: none -> 176 us  [the longest x4 160 us: per_device(): from_left = lax.ppermute(from_left, 'row', ahead)]
    all_gather x1, waiting for transfers between devices: 141 us -> 0.01 us  [per_device(): lax.all_gather(int_low, 'col', axis=1, tiled=True)]
    all_gather x1 -> x0, waiting for transfers between devices: 100 us -> none  [per_device(): amp_strip = lax.all_gather(compact, 'row', axis=2, tiled=True)]
    all_gather x2 -> x0, local copies, waits for them, and re-layouts: 86.2 us -> none  [per_device(): amp_strip = lax.all_gather(compact, 'row', axis=2, tiled=True)]
    dynamic_update_slice x0 -> x8, local copies, waits for them, and re-layouts: none -> 45 us  [the longest x4 22.4 us: per_device(): lax.dynamic_update_slice_in_dim(whole, from_left, (index - step) % size *...]
    broadcast_in_dim x0 -> x1, local copies, waits for them, and re-layouts: none -> 17.4 us  [per_device(): jnp.zeros((*compact.shape[:2], size * width, *compact.shape[2 + 1:]), com...]
    ppermute x0 -> x7, starting transfers between devices: none -> 9.67 us  [the longest x3 8.47 us: per_device(): from_right = lax.ppermute(from_right, 'row', left)]
    unnamed x6 -> x12, local copies, waits for them, and re-layouts: 25.7 us -> 25.6 us
  transfers between devices with their start and end apart: 3 -> 9, of which waited for: 3 -> 7; matrix products, arithmetic and copies ran while one was open for 21% -> 19% of each run, Pallas kernels for 0% -> 0%
where the time goes in v1:
time: 760 us; the launch traced here: 751 us
  waiting for transfers between devices  356 us (47%)
  local copies, waits for them, and re-layouts  165 us (22%)
  blocking collectives  102 us (13%)
  matrix products  74.6 us (10%)
  other arithmetic  24.2 us (3%)
  starting transfers between devices  15.5 us (2%)
  between operations  13.7 us (2%)
    all_to_all x1, waiting for transfers between devices, per_device(): lax.all_to_all(stacked, 'col', split_axis=0, concat_axis=1, tiled=True)  181 us
    ppermute x4, waiting for transfers between devices, per_device(): from_left = lax.ppermute(from_left, 'row', ahead)  160 us
    all_to_all x1, blocking collectives, per_device(): lax.all_to_all(pieces, 'row', split_axis=2, concat_axis=1, tiled=True)  102 us
    dot_general x1, matrix products, per_device(): jnp.dot(lax.all_gather(int_low, 'col', axis=1, tiled=True), amp_full, pre...  44 us
    dot_general x1, matrix products, per_device(): jnp.einsum('kt,kjrb->tjrb', selector, amp_strip)  30.6 us
    dot_general x1, local copies, waits for them, and re-layouts, per_device(): jnp.einsum('kt,kjrb->tjrb', selector, amp_strip)  30 us
    unnamed x12, local copies, waits for them, and re-layouts  25.6 us
    dynamic_update_slice x4, local copies, waits for them, and re-layouts, per_device(): lax.dynamic_update_slice_in_dim(whole, from_left, (index - step) % size *...  22.4 us
  transfers between devices with their start and end apart: 9, of which 7 were waited for; matrix products, arithmetic and copies ran while one was open for 19% of the time, Pallas kernels for 0%

profile of v1, /device:TPU:0, one launch (start us, length us, event | category | flops | bytes accessed | tf_op | source)
XLA Modules:
  0.0 750.6 jit_solution(1522510357664279216)
XLA Ops:
  6.5 0.0 all-gather.2.cloned.1.call-start
  6.5 20.5 %copy.35 = f32[1024,1,2048]{0,2,1:T(8,128)} copy(f32[1024,1,2048]{2,1,0:T(1,128)} %param.5) | data formatting | bytes 16777216 | tf_op args[0]
  27.1 6.0 bitcast_convert_fusion
  33.1 0.0 all-gather.2.cloned.1.call-update
  33.2 7.1 convert_element_type.11
  40.3 0.0 copy-start.4
  40.3 4.8 copy.50
  45.1 0.0 copy-done.4
  45.1 3.7 gather_fusion
  48.9 0.6 collective-permute-start
  49.4 2.9 collective-permute-start.1
  52.3 66.0 %collective-permute-done = bf16[3,256,1,2048]{3,1,0,2:T(8,128)(2,1)S(1)} collective-permute-done((bf16[3,256,1,2048]{3,1,0,2:T(8,128)(2,1)S(1)}, bf16[3,256,1,2048]{3,1,0,2:T(8,128)(2,1)S(1)}, u32[]{:S(2)}, u32[]{:S(2)}) %collective-permute-start) | collective-permute-done | bytes 3145760 | tf_op jit(solution)/shard_map/ppermute | solution.py:36
  118.3 0.0 copy-start
  118.3 0.5 collective-permute-start.2
  118.8 0.9 collective-permute-done.1
  119.7 0.2 copy-done
  120.0 3.0 collective-permute-start.3
  122.9 64.1 %collective-permute-done.2 = bf16[3,256,1,2048]{3,1,0,2:T(8,128)(2,1)} collective-permute-done((bf16[3,256,1,2048]{3,1,0,2:T(8,128)(2,1)S(1)}, bf16[3,256,1,2048]{3,1,0,2:T(8,128)(2,1)}, u32[]{:S(2)}, u32[]{:S(2)}) %collective-permute-start.2) | collective-permute-done | bytes 3145760 | tf_op jit(solution)/shard_map/ppermute | solution.py:36
  187.0 0.0 collective-permute-start.4
  187.0 17.4 %broadcast_in_dim.42 = bf16[3,256,8,2048]{3,0,2,1:T(4,128)(2,1)} broadcast(bf16[]{:T(256)} %constant.58.clone.1), dimensions={} | broadcast | bytes 25165826 | tf_op jit(solution)/shard_map/broadcast_in_dim | solution.py:31
  204.4 0.0 copy-start.1
  204.4 4.7 copy_dynamic-update-slice_fusion.7
  209.1 0.0 collective-permute-done.3
  209.1 2.6 collective-permute-start.5
  211.7 0.0 copy-done.1
  211.7 4.7 copy_dynamic-update-slice_fusion.6
  216.4 19.6 %collective-permute-done.4 = bf16[3,256,1,2048]{3,1,0,2:T(8,128)(2,1)} collective-permute-done((bf16[3,256,1,2048]{3,1,0,2:T(8,128)(2,1)}, bf16[3,256,1,2048]{3,1,0,2:T(8,128)(2,1)}, u32[]{:S(2)}, u32[]{:S(2)}) %collective-permute-start.4) | collective-permute-done | bytes 3145760 | tf_op jit(solution)/shard_map/ppermute | solution.py:36
  236.1 0.2 collective-permute-start.6
  236.2 6.6 copy_dynamic-update-slice_fusion.5
  242.8 6.5 copy_dynamic-update-slice_fusion.4
  249.3 6.5 copy_dynamic-update-slice_fusion.3
  255.8 6.5 copy_dynamic-update-slice_fusion.2
  262.4 14.7 %collective-permute-done.5 = bf16[3,256,1,2048]{3,1,0,2:T(8,128)(2,1)S(1)} collective-permute-done((bf16[3,256,1,2048]{3,1,0,2:T(8,128)(2,1)}, bf16[3,256,1,2048]{3,1,0,2:T(8,128)(2,1)S(1)}, u32[]{:S(2)}, u32[]{:S(2)}) %collective-permute-start.5) | collective-permute-done | bytes 3145760 | tf_op jit(solution)/shard_map/ppermute | solution.py:41
  277.1 4.8 copy_dynamic-update-slice_fusion.1
  281.9 10.3 %collective-permute-done.6 = bf16[3,256,1,2048]{3,1,0,2:T(8,128)(2,1)S(1)} collective-permute-done((bf16[3,256,1,2048]{3,1,0,2:T(8,128)(2,1)}, bf16[3,256,1,2048]{3,1,0,2:T(8,128)(2,1)S(1)}, u32[]{:S(2)}, u32[]{:S(2)}) %collective-permute-start.6) | collective-permute-done | bytes 3145760 | tf_op jit(solution)/shard_map/ppermute | solution.py:36
  292.2 4.6 copy_dynamic-update-slice_fusion
  296.9 30.6 %fusion.4 = bf16[4,256,8,2048]{3,0,2,1:T(4,128)(2,1)} fusion(bf16[3,256,8,2048]{3,0,2,1:T(4,128)(2,1)} %copy_dynamic-update-slice_fusion, s32[3]{0:T(128)S(1)} %fusion.8), kind=kOutput, calls=%fused_computation.25 | convolution fusion | flops 100663312 | bytes 58720268 | tf_op jit(solution)/shard_map/kt,kjrb->tjrb/dot_general | solution.py:49
  327.5 30.0 %copy.44 = bf16[4,256,8,2048]{3,2,1,0:T(8,128)(2,1)} copy(bf16[4,256,8,2048]{3,0,2,1:T(4,128)(2,1)} %fusion.4) | data formatting | bytes 67108864 | tf_op jit(solution)/shard_map/kt,kjrb->tjrb/dot_general | solution.py:49
  357.4 0.0 all-gather.2.cloned.1.call-done
  357.4 44.0 %fusion.9 = f32[2048,1024]{1,0:T(8,128)} fusion(bf16[8192,2048]{1,0:T(8,128)(2,1)} %bitcast.49, bf16[1024,8192]{0,1:T(8,128)(2,1)} %all-gather.2.cloned.1.call-done), kind=kOutput, calls=%fused_computation.29 | convolution fusion | flops 34359738368 | bytes 58720256 | tf_op jit(solution)/shard_map/dot_general | solution.py:50
  401.5 9.2 %copy.45 = f32[1024,256,8]{1,0,2:T(8,128)} copy(f32[1024,256,8]{0,2,1:T(8,128)} %bitcast.47) | data formatting | bytes 16777216 | tf_op jit(solution)/shard_map/reshape | solution.py:55
  410.7 101.6 %all_to_all.34 = f32[1024,256,8]{1,0,2:T(8,128)S(1)} all-to-all(f32[1024,256,8]{1,0,2:T(8,128)} %copy.45), channel_id=1, replica_groups=mesh['row'=8,'col'=4] {'row'}, dimensions={2} | all-to-all | bytes 16777216 | tf_op jit(solution)/shard_map/all_to_all | solution.py:56
  512.4 8.1 %copy.46 = f32[1024,256,8]{1,2,0:T(8,128)} copy(f32[1024,256,8]{1,0,2:T(8,128)S(1)} %all_to_all.34) | data formatting | bytes 16777216 | tf_op jit(solution)/shard_map/all_to_all | solution.py:56
  520.5 0.0 copy-start.2
  520.5 0.0 copy-start.3
  520.5 5.8 all-to-all-start.1
  526.2 0.0 copy-done.2
  526.3 0.3 reshape.52
  526.6 0.4 dynamic-slice_reduce_fusion
  526.9 0.0 copy-done.3
  527.0 0.5 select_reduce_fusion.1
  527.4 0.9 select_reduce_fusion
  528.4 180.7 %all-to-all-done.1 = f32[4,2048,256]{2,1,0:T(8,128)} async-done(((f32[4,2048,256]{2,1,0:T(8,128)}), f32[4,2048,256]{2,1,0:T(8,128)}, u32[]{:S(2)}, u32[]{:S(2)}) %all-to-all-start.1) | async-done | bytes 8388640 | tf_op jit(solution)/shard_map/all_to_all | solution.py:60
  709.0 4.4 copy.51
  713.5 9.6 %fusion.2 = f32[1024,1,2048]{0,2,1:T(8,128)} fusion(f32[2048,1024]{1,0:T(8,128)S(1)} %bitcast.48, f32[2048,1024]{1,0:T(8,128)} %fusion.9, f32[1024,1,2048]{0,2,1:T(8,128)} %copy.35, f32[2048]{0:T(1024)S(1)} %select_reduce_fusion, f32[1024]{0:T(1024)S(1)} %select_reduce_fusion.1), kind=kLoop, calls=%fused_computation.4 | loop fusion | flops 10485760 | bytes 33566720 | tf_op jit(solution)/shard_map/broadcast_in_dim | solution.py:70
  723.1 20.5 %copy.48 = f32[1024,1,2048]{2,1,0:T(1,128)} copy(f32[1024,1,2048]{0,2,1:T(8,128)} %fusion.2) | data formatting | bytes 16777216 | tf_op jit(solution)/shard_map/broadcast_in_dim | solution.py:70
  (4 shorter events, 0.0 us)
Async XLA Ops:
  6.5 350.9 %all-gather.2.cloned.1.call-start = ((), (), s32[]{:S(2)}) async-start(), calls=%async_computation.2 | async-start | bytes 20971520 | tf_op jit(solution)/shard_map/all_gather | solution.py:51
  40.3 4.8 copy-start.4
  48.9 69.5 %collective-permute-start = (bf16[3,256,1,2048]{3,1,0,2:T(8,128)(2,1)S(1)}, bf16[3,256,1,2048]{3,1,0,2:T(8,128)(2,1)S(1)}, u32[]{:S(2)}, u32[]{:S(2)}) collective-permute-start(bf16[3,256,1,2048]{3,1,0,2:T(8,128)(2,1)S(1)} %bitcast.52), channel_id=1, source_target_pairs={{0,4},{4,8},{8,12},{12,16},{16,20},{20,24},{24,28},{28,0},{1,5},{5... | collective-permute-start | bytes 9437192 | tf_op jit(solution)/shard_map/ppermute | solution.py:36
  49.4 70.3 %collective-permute-start.1 = (bf16[3,256,1,2048]{3,1,0,2:T(8,128)(2,1)S(1)}, bf16[3,256,1,2048]{3,1,0,2:T(8,128)(2,1)}, u32[]{:S(2)}, u32[]{:S(2)}) collective-permute-start(bf16[3,256,1,2048]{3,1,0,2:T(8,128)(2,1)S(1)} %bitcast.53), channel_id=1, source_target_pairs={{0,28},{4,0},{8,4},{12,8},{16,12},{20,16},{24,20},{28,24},{1,29},{... | collective-permute-start | bytes 9437192 | tf_op jit(solution)/shard_map/ppermute | solution.py:41
  118.3 1.6 copy-start
  118.3 68.7 %collective-permute-start.2 = (bf16[3,256,1,2048]{3,1,0,2:T(8,128)(2,1)S(1)}, bf16[3,256,1,2048]{3,1,0,2:T(8,128)(2,1)}, u32[]{:S(2)}, u32[]{:S(2)}) collective-permute-start(bf16[3,256,1,2048]{3,1,0,2:T(8,128)(2,1)S(1)} %collective-permute-done), channel_id=1, source_target_pairs={{0,4},{4,8},{8,12},{12,16},{16,20},{20,24},{24,28},{28,0},{1,5},{5... | collective-permute-start | bytes 9437192 | tf_op jit(solution)/shard_map/ppermute | solution.py:36
  120.0 89.2 %collective-permute-start.3 = (bf16[3,256,1,2048]{3,1,0,2:T(8,128)(2,1)}, bf16[3,256,1,2048]{3,1,0,2:T(8,128)(2,1)}, u32[]{:S(2)}, u32[]{:S(2)}) collective-permute-start(bf16[3,256,1,2048]{3,1,0,2:T(8,128)(2,1)} %collective-permute-done.1), channel_id=1, source_target_pairs={{0,28},{4,0},{8,4},{12,8},{16,12},{20,16},{24,20},{28,24},{1,29},{... | collective-permute-start | bytes 9437192 | tf_op jit(solution)/shard_map/ppermute | solution.py:41
  187.0 49.0 %collective-permute-start.4 = (bf16[3,256,1,2048]{3,1,0,2:T(8,128)(2,1)}, bf16[3,256,1,2048]{3,1,0,2:T(8,128)(2,1)}, u32[]{:S(2)}, u32[]{:S(2)}) collective-permute-start(bf16[3,256,1,2048]{3,1,0,2:T(8,128)(2,1)} %collective-permute-done.2), channel_id=1, source_target_pairs={{0,4},{4,8},{8,12},{12,16},{16,20},{20,24},{24,28},{28,0},{1,5},{5... | collective-permute-start | bytes 9437192 | tf_op jit(solution)/shard_map/ppermute | solution.py:36
  204.4 7.3 copy-start.1
  209.1 68.0 %collective-permute-start.5 = (bf16[3,256,1,2048]{3,1,0,2:T(8,128)(2,1)}, bf16[3,256,1,2048]{3,1,0,2:T(8,128)(2,1)S(1)}, u32[]{:S(2)}, u32[]{:S(2)}) collective-permute-start(bf16[3,256,1,2048]{3,1,0,2:T(8,128)(2,1)} %collective-permute-done.3), channel_id=1, source_target_pairs={{0,28},{4,0},{8,4},{12,8},{16,12},{20,16},{24,20},{28,24},{1,29},{... | collective-permute-start | bytes 9437192 | tf_op jit(solution)/shard_map/ppermute | solution.py:41
  236.1 56.2 %collective-permute-start.6 = (bf16[3,256,1,2048]{3,1,0,2:T(8,128)(2,1)}, bf16[3,256,1,2048]{3,1,0,2:T(8,128)(2,1)S(1)}, u32[]{:S(2)}, u32[]{:S(2)}) collective-permute-start(bf16[3,256,1,2048]{3,1,0,2:T(8,128)(2,1)} %collective-permute-done.4), channel_id=1, source_target_pairs={{0,4},{4,8},{8,12},{12,16},{16,20},{20,24},{24,28},{28,0},{1,5},{5... | collective-permute-start | bytes 9437192 | tf_op jit(solution)/shard_map/ppermute | solution.py:36
  520.5 5.8 copy-start.2
  520.5 6.5 copy-start.3
  520.5 188.6 %all-to-all-start.1 = ((f32[4,2048,256]{2,1,0:T(8,128)}), f32[4,2048,256]{2,1,0:T(8,128)}, u32[]{:S(2)}, u32[]{:S(2)}) async-start(f32[4,2048,256]{2,1,0:T(8,128)} %bitcast.50), calls=%async_computation.1 | async-start | bytes 16777216 | tf_op jit(solution)/shard_map/all_to_all | solution.py:60
Sparse Core Ops, SparseCore 0:
  33.3 289.4 all-gather.1
